TPU v7x, 32 devices: a whole 2x2x4 slice. The times are simulated.
32 devices in a mesh: rep: 2 (over x), blk: 16 (over z, y, core).
Axes of the slice: x: 2, y: 2, z: 4, core: 2. Of those that a mesh axis runs over, the one named last changes fastest.
Arguments:
- features: bfloat16 [4096, 512], P(('rep', 'blk')), may hold values from -6 to 6
- weight: bfloat16 [512, 512], replicated, may hold values from -0.25 to 0.25
- tile_values: bfloat16 [2, 16, 16, 2, 128, 128], P('rep', 'blk'), as said below
- tile_list: int32 [2, 16, 16, 2], P('rep', 'blk'), may hold values from -1 to 1, as said below
- train_mask: int32 [4096], P(('rep', 'blk')), may hold values 0 or 1
- cotangent: bfloat16 [4096, 512], P(('rep', 'blk')), may hold values from -6 to 6
Outputs:
- activated: bfloat16 [4096, 512], P(('rep', 'blk'))
- weight_grad: float32 [512, 512], replicated
- feature_grad: bfloat16 [4096, 512], P(('rep', 'blk'))
Inputs may be any that keep to these rules, and one draw needn't show every extreme that they name: `tile_list`: -1 marks an empty slot; 0 or 1 names the half h whose tile [r, b, j, h] is nonempty; the two slots of a pair never name the same half. The graph is undirected: block (u, v) of A is nonempty exactly when block (v, u) is, and every block (u, u) is nonempty. How many nonempty tiles a device holds differs from device to device. `tile_values`: the tile of block (u, v) is the transpose of the tile of block (v, u), so A is symmetric.
All inputs are finite; a program needn't handle non-finite values. No bound on the sum of `train_mask` on one device may be relied on, other than what follows from the above.
Results may differ from a plain program's by a relative error of at most 0.014.
Values may be sent and summed in bfloat16 or wider, within the bound.
A program may use at most 128 MiB of HBM per device.

v0:
```python
import math
import jax
import jax.numpy as jnp
from jax import lax
from jax.sharding import PartitionSpec as P

GELU_SCALE = math.sqrt(2.0 / math.pi)


def activation(pre_act):
    inner = GELU_SCALE * (pre_act + 0.044715 * pre_act * pre_act * pre_act)
    tanh_part = jnp.tanh(inner)
    act_value = 0.5 * pre_act * (1.0 + tanh_part)
    act_slope = 0.5 * (1.0 + tanh_part) + 0.5 * pre_act * (
        1.0 - tanh_part * tanh_part
    ) * GELU_SCALE * (1.0 + 3.0 * 0.044715 * pre_act * pre_act)
    return (act_value, act_slope)


def on_device(features, weight, tile_values, tile_list, train_mask, cotangent):
    tile_rows = features.shape[0]
    feat_width = features.shape[1]
    pair_list = tile_list[0, 0]
    presence = jnp.stack(
        [jnp.any(pair_list == 0, axis=1), jnp.any(pair_list == 1, axis=1)], axis=1
    ).astype(jnp.bfloat16)
    masked = tile_values[0, 0] * presence[:, :, None, None]
    projected = jnp.dot(features, weight, preferred_element_type=jnp.float32).astype(jnp.bfloat16)

    def apply_tiles(incoming):
        shard_count = incoming.shape[0] // tile_rows
        return jnp.einsum(
            "jhst,jtf->hsf",
            masked,
            incoming.reshape(shard_count, tile_rows, feat_width),
            preferred_element_type=jnp.float32,
        )

    partial_value = apply_tiles(lax.all_gather(projected, "blk", axis=0, tiled=True))
    summed = lax.psum_scatter(
        partial_value.reshape(2 * tile_rows, feat_width).astype(jnp.bfloat16),
        "rep",
        scatter_dimension=0,
        tiled=True,
    ).astype(jnp.float32)
    act_value, act_slope = activation(summed)
    activated = act_value.astype(jnp.bfloat16)
    grad_z = (
        cotangent.astype(jnp.float32) * train_mask.astype(jnp.float32)[:, None] * act_slope
    ).astype(jnp.bfloat16)
    folded = apply_tiles(lax.all_gather(grad_z, "blk", axis=0, tiled=True))
    prop_sums = lax.psum_scatter(
        folded.reshape(2 * tile_rows, feat_width).astype(jnp.bfloat16),
        "rep",
        scatter_dimension=0,
        tiled=True,
    )
    local_term = lax.dot_general(
        features, prop_sums, (((0,), (0,)), ((), ())), preferred_element_type=jnp.float32
    )
    weight_grad = lax.psum(local_term, ("rep", "blk"))
    feature_grad = lax.dot_general(
        prop_sums, weight, (((1,), (1,)), ((), ())), preferred_element_type=jnp.float32
    ).astype(jnp.bfloat16)
    return (activated, weight_grad, feature_grad)


def solution(mesh):
    in_specs = (
        P(("rep", "blk"), None),
        P(),
        P("rep", "blk", None, None, None, None),
        P("rep", "blk", None, None),
        P(("rep", "blk")),
        P(("rep", "blk"), None),
    )
    out_specs = (P(("rep", "blk"), None), P(), P(("rep", "blk"), None))
    return jax.shard_map(
        on_device, mesh=mesh, in_specs=in_specs, out_specs=out_specs, check_vma=False
    )
```

profile of v0, /device:TPU:0, one launch (start us, length us, event | category | flops | bytes accessed | tf_op | source)
XLA Modules:
  0.0 271.8 jit_solution(10915368503565097484)
XLA Ops:
  7.2 0.0 copy-start
  7.2 0.0 all-gather.3.cloned.1.call-start
  7.2 1.0 copy-done
  8.2 1.8 convolution_convert_fusion.1
  10.0 0.0 all-gather.3.cloned.1.call-update
  10.0 0.0 reduce-scatter.3.cloned.1.call-start
  10.1 0.7 compare_reduce_fusion.1
  10.8 0.1 copy.9
  10.9 1.4 bitcast_multiply_fusion
  12.3 0.0 copy-start.4
  12.3 0.0 copy-start.3
  12.3 42.6 %all-gather.3.cloned.1.call-done = bf16[2048,512]{1,0:T(8,128)(2,1)} async-done(((bf16[128,512]{1,0:T(8,128)(2,1)}), bf16[2048,512]{1,0:T(8,128)(2,1)}) %all-gather.3.cloned.1.call-update) | async-done | bytes 2097168 | tf_op jit(solution)/shard_map/all_gather | solution.py:39
  54.9 3.0 %fusion = bf16[256,512]{1,0:T(8,128)(2,1)} fusion(bf16[256,16,128]{2,0,1:T(8,128)(2,1)S(1)} %bitcast.29, bf16[16,128,512]{2,1,0:T(8,128)(2,1)} %bitcast.33), kind=kOutput, calls=%fused_computation.3 | convolution fusion | flops 537001984 | bytes 3407872 | tf_op jit(solution)/shard_map/jhst,jtf->hsf/dot_general | solution.py:32
  57.9 0.0 reduce-scatter.3.cloned.1.call-update
  58.0 0.0 all-gather.5.cloned.1.call-start
  58.0 0.0 copy-done.4
  58.0 10.6 %reduce-scatter.3.cloned.1.call-done = bf16[128,512]{1,0:T(8,128)(2,1)} async-done(((bf16[256,512]{1,0:T(8,128)(2,1)}), bf16[128,512]{1,0:T(8,128)(2,1)}) %reduce-scatter.3.cloned.1.call-update) | async-done | bytes 131088 | tf_op jit(solution)/shard_map/reduce_scatter | solution.py:40
  68.6 0.0 copy-done.3
  68.6 1.8 fusion.9
  70.4 0.0 all-gather.5.cloned.1.call-update
  70.4 0.0 reduce-scatter.5.cloned.1.call-start
  70.5 42.3 %all-gather.5.cloned.1.call-done = bf16[2048,512]{1,0:T(8,128)(2,1)} async-done(((bf16[128,512]{1,0:T(8,128)(2,1)}), bf16[2048,512]{1,0:T(8,128)(2,1)}) %all-gather.5.cloned.1.call-update) | async-done | bytes 2097168 | tf_op jit(solution)/shard_map/all_gather | solution.py:51
  112.8 3.0 %fusion.1 = bf16[256,512]{1,0:T(8,128)(2,1)} fusion(bf16[256,16,128]{2,0,1:T(8,128)(2,1)S(1)} %bitcast.30, bf16[16,128,512]{2,1,0:T(8,128)(2,1)} %bitcast.34), kind=kOutput, calls=%fused_computation.4 | convolution fusion | flops 537001984 | bytes 3407872 | tf_op jit(solution)/shard_map/jhst,jtf->hsf/dot_general | solution.py:32
  115.8 0.0 reduce-scatter.5.cloned.1.call-update
  115.8 0.0 all-reduce.2.cloned.1.call-start
  115.9 10.6 %reduce-scatter.5.cloned.1.call-done = bf16[128,512]{1,0:T(8,128)(2,1)} async-done(((bf16[256,512]{1,0:T(8,128)(2,1)}), bf16[128,512]{1,0:T(8,128)(2,1)}) %reduce-scatter.5.cloned.1.call-update) | async-done | bytes 131088 | tf_op jit(solution)/shard_map/reduce_scatter | solution.py:52
  126.5 0.0 copy-done.1
  126.5 2.3 convolution_bitcast_fusion
  128.8 0.0 all-reduce.2.cloned.1.call-update
  128.8 1.0 convolution_convert_fusion
  129.7 133.0 %all-reduce.2.cloned.1.call-done = f32[512,512]{0,1:T(8,128)} async-done(((f32[512,512]{0,1:T(8,128)}), f32[512,512]{0,1:T(8,128)}) %all-reduce.2.cloned.1.call-update) | async-done | bytes 1048592 | tf_op jit(solution)/shard_map/psum | solution.py:61
  262.7 2.5 copy.10
  (5 shorter events, 0.0 us)
Async XLA Ops:
  7.2 1.0 copy-start
  7.2 47.8 %all-gather.3.cloned.1.call-start = ((), (), s32[]{:S(2)}) async-start(), calls=%async_computation.2 | async-start | bytes 2228224 | tf_op jit(solution)/shard_map/all_gather | solution.py:39
  10.0 58.6 %reduce-scatter.3.cloned.1.call-start = ((), (), s32[]{:S(2)}) async-start(), calls=%async_computation.3 | async-start | bytes 393216 | tf_op jit(solution)/shard_map/reduce_scatter | solution.py:40
  12.3 45.8 %copy-start.4 = (s32[128]{0:T(128)S(1)}, s32[128]{0:T(128)}, u32[]{:S(2)}) copy-start(s32[128]{0:T(128)} %param.10) | copy-start | bytes 1540
  12.3 56.3 %copy-start.3 = (bf16[128,512]{1,0:T(8,128)(2,1)S(1)}, bf16[128,512]{1,0:T(8,128)(2,1)}, u32[]{:S(2)}) copy-start(bf16[128,512]{1,0:T(8,128)(2,1)} %param.11) | copy-start | bytes 393220
  58.0 54.9 %all-gather.5.cloned.1.call-start = ((), (), s32[]{:S(2)}) async-start(), calls=%async_computation.4 | async-start | bytes 2228224 | tf_op jit(solution)/shard_map/all_gather | solution.py:51
  70.4 56.1 %copy-start.1 = (bf16[128,512]{1,0:T(8,128)(2,1)S(1)}, bf16[128,512]{1,0:T(8,128)(2,1)}, u32[]{:S(2)}) copy-start(bf16[128,512]{1,0:T(8,128)(2,1)} %param.6) | copy-start | bytes 393220
  70.4 56.0 %reduce-scatter.5.cloned.1.call-start = ((), (), s32[]{:S(2)}) async-start(), calls=%async_computation.5 | async-start | bytes 393216 | tf_op jit(solution)/shard_map/reduce_scatter | solution.py:52
  115.8 146.9 %all-reduce.2.cloned.1.call-start = ((), (), s32[]{:S(2)}) async-start(), calls=%async_computation.6 | async-start | bytes 2097152 | tf_op jit(solution)/shard_map/psum | solution.py:61
  126.5 2.3 copy-start.2
Sparse Core Ops, SparseCore 0:
  10.7 44.1 all-gather.2
  58.1 10.4 reduce-scatter.2
  71.3 41.4 all-gather.4
  116.0 10.4 reduce-scatter.4
  132.1 130.6 all-reduce.1
where the time goes:
time: 272 us
  waiting for transfers between devices  239 us (88%)
  between operations  13.8 us (5%)
  matrix products  11 us (4%)
  other arithmetic  3.89 us (1%)
  local copies, waits for them, and re-layouts  3.64 us (1%)
    psum x1, waiting for transfers between devices, on_device(): weight_grad = lax.psum(local_term, ('rep', 'blk'))  133 us
    all_gather x1, waiting for transfers between devices, on_device(): lax.all_gather(projected, 'blk', axis=0, tiled=True)  42.6 us
    all_gather x1, waiting for transfers between devices, on_device(): folded = apply_tiles(lax.all_gather(grad_z, 'blk', axis=0, tiled=True))  42.3 us
    reduce_scatter x1, waiting for transfers between devices, on_device(): lax.psum_scatter(folded.reshape(2 * tile_rows, feat_width).astype(jnp.bfl...  10.6 us
    reduce_scatter x1, waiting for transfers between devices, on_device(): lax.psum_scatter(partial_value.reshape(2 * tile_rows, feat_width).astype(...  10.6 us
    dot_general x2, matrix products, apply_tiles(): jnp.einsum('jhst,jtf->hsf', masked, incoming.reshape(shard_count, tile_ro...  6 us
  transfers between devices with their start and end apart: 5, of which 5 were waited for; matrix products, arithmetic and copies ran while one was open for 1% of the time, Pallas kernels for 0%

commit v1 on v0

--- a/solution.py
+++ b/solution.py
@@ -5,6 +5,18 @@
 from jax.sharding import PartitionSpec as P
 
 GELU_SCALE = math.sqrt(2.0 / math.pi)
+
+
+def collect(x, axis, dim):
+    ways, here = (lax.axis_size(axis), lax.axis_index(axis))
+    grown, reach = (x, 1)
+    while reach < ways:
+        theirs = lax.ppermute(grown, axis, [(d, d ^ reach) for d in range(ways)])
+        mine_first = jnp.concatenate([grown, theirs], axis=dim)
+        theirs_first = jnp.concatenate([theirs, grown], axis=dim)
+        grown = jnp.where(here & reach == 0, mine_first, theirs_first)
+        reach = 2 * reach
+    return grown
 
 
 def activation(pre_act):
@@ -48,7 +60,7 @@
     grad_z = (
         cotangent.astype(jnp.float32) * train_mask.astype(jnp.float32)[:, None] * act_slope
     ).astype(jnp.bfloat16)
-    folded = apply_tiles(lax.all_gather(grad_z, "blk", axis=0, tiled=True))
+    folded = apply_tiles(collect(grad_z, "blk", 0))
     prop_sums = lax.psum_scatter(
         folded.reshape(2 * tile_rows, feat_width).astype(jnp.bfloat16),
         "rep",

time: 272 us -> 301 us (1.11)
  waiting for transfers between devices: 239 us -> 263 us
  starting transfers between devices: 0.21 us -> 5.69 us
    ppermute x0 -> x4, waiting for transfers between devices: none -> 64.4 us  [collect(): theirs = lax.ppermute(grown, axis, [(d, d ^ reach) for d in range(ways)])]
    all_gather x1 -> x0, waiting for transfers between devices: 42.3 us -> none  [on_device(): folded = apply_tiles(lax.all_gather(grad_z, 'blk', axis=0, tiled=True))]
    ppermute x0 -> x4, starting transfers between devices: none -> 5.53 us  [collect(): theirs = lax.ppermute(grown, axis, [(d, d ^ reach) for d in range(ways)])]
  transfers between devices with their start and end apart: 5 -> 8, of which waited for: 5 -> 8; matrix products, arithmetic and copies ran while one was open for 1% -> 1% of each run, Pallas kernels for 0% -> 0%
where the time goes in v1:
time: 301 us; the launch traced here: 300 us
  waiting for transfers between devices  263 us (87%)
  between operations  13.9 us (5%)
  matrix products  9.43 us (3%)
  starting transfers between devices  5.69 us (2%)
  other arithmetic  5.16 us (2%)
  local copies, waits for them, and re-layouts  3.65 us (1%)
    psum x1, waiting for transfers between devices, on_device(): weight_grad = lax.psum(local_term, ('rep', 'blk'))  133 us
    ppermute x4, waiting for transfers between devices, collect(): theirs = lax.ppermute(grown, axis, [(d, d ^ reach) for d in range(ways)])  64.4 us
    all_gather x1, waiting for transfers between devices, on_device(): lax.all_gather(projected, 'blk', axis=0, tiled=True)  42.6 us
    reduce_scatter x1, waiting for transfers between devices, on_device(): lax.psum_scatter(folded.reshape(2 * tile_rows, feat_width).astype(jnp.bfl...  11.8 us
    reduce_scatter x1, waiting for transfers between devices, on_device(): lax.psum_scatter(partial_value.reshape(2 * tile_rows, feat_width).astype(...  10.6 us
  transfers between devices with their start and end apart: 8, of which 8 were waited for; matrix products, arithmetic and copies ran while one was open for 1% of the time, Pallas kernels for 0%

profile of v1, /device:TPU:0, one launch (start us, length us, event | category | flops | bytes accessed | tf_op | source)
XLA Modules:
  0.0 300.3 jit_solution(9487401133238656369)
XLA Ops:
  7.2 0.0 all-gather.2.cloned.1.call-start
  7.2 1.0 copy-done
  8.2 1.8 convolution_convert_fusion.1
  10.0 0.0 all-gather.2.cloned.1.call-update
  10.0 0.0 reduce-scatter.3.cloned.1.call-start
  10.1 0.7 compare_reduce_fusion.1
  10.8 0.1 copy.9
  10.9 1.4 bitcast_multiply_fusion
  12.3 42.6 %all-gather.2.cloned.1.call-done = bf16[2048,512]{1,0:T(8,128)(2,1)} async-done(((bf16[128,512]{1,0:T(8,128)(2,1)}), bf16[2048,512]{1,0:T(8,128)(2,1)}) %all-gather.2.cloned.1.call-update) | async-done | bytes 2097168 | tf_op jit(solution)/shard_map/all_gather | solution.py:51
  54.9 3.0 fusion
  57.9 0.0 reduce-scatter.3.cloned.1.call-update
  58.0 0.0 reduce-scatter.5.cloned.1.call-start
  58.0 10.6 %reduce-scatter.3.cloned.1.call-done = bf16[128,512]{1,0:T(8,128)(2,1)} async-done(((bf16[256,512]{1,0:T(8,128)(2,1)}), bf16[128,512]{1,0:T(8,128)(2,1)}) %reduce-scatter.3.cloned.1.call-update) | async-done | bytes 131088 | tf_op jit(solution)/shard_map/reduce_scatter | solution.py:52
  68.6 1.8 fusion.9
  70.4 1.3 collective-permute-done
  71.7 0.1 maximum_select_fusion.3
  71.8 1.5 collective-permute-start.1
  73.3 6.9 %collective-permute-done.1 = bf16[256,512]{1,0:T(8,128)(2,1)S(1)} collective-permute-done((bf16[256,512]{1,0:T(8,128)(2,1)S(1)}, bf16[256,512]{1,0:T(8,128)(2,1)S(1)}, u32[]{:S(2)}, u32[]{:S(2)}) %collective-permute-start.1) | collective-permute-done | bytes 262176 | tf_op jit(solution)/shard_map/ppermute | solution.py:14
  80.2 0.2 maximum_select_fusion.2
  80.4 1.6 collective-permute-start.2
  82.0 11.6 %collective-permute-done.2 = bf16[512,512]{1,0:T(8,128)(2,1)S(1)} collective-permute-done((bf16[512,512]{1,0:T(8,128)(2,1)S(1)}, bf16[512,512]{1,0:T(8,128)(2,1)S(1)}, u32[]{:S(2)}, u32[]{:S(2)}) %collective-permute-start.2) | collective-permute-done | bytes 524320 | tf_op jit(solution)/shard_map/ppermute | solution.py:14
  93.6 0.5 maximum_select_fusion.1
  94.1 2.5 collective-permute-start.3
  96.5 44.5 %collective-permute-done.3 = bf16[1024,512]{1,0:T(8,128)(2,1)S(1)} collective-permute-done((bf16[1024,512]{1,0:T(8,128)(2,1)S(1)}, bf16[1024,512]{1,0:T(8,128)(2,1)S(1)}, u32[]{:S(2)}, u32[]{:S(2)}) %collective-permute-start.3) | collective-permute-done | bytes 1048608 | tf_op jit(solution)/shard_map/ppermute | solution.py:14
  141.0 0.6 maximum_select_fusion
  141.6 1.4 fusion.1
  143.0 0.0 all-reduce.2.cloned.1.call-start
  143.1 11.8 %reduce-scatter.5.cloned.1.call-done = bf16[128,512]{1,0:T(8,128)(2,1)} async-done(((bf16[256,512]{1,0:T(8,128)(2,1)}), bf16[128,512]{1,0:T(8,128)(2,1)}) %reduce-scatter.5.cloned.1.call-update) | async-done | bytes 131088 | tf_op jit(solution)/shard_map/reduce_scatter | solution.py:64
  154.9 2.3 convolution_bitcast_fusion
  157.2 1.0 convolution_convert_fusion
  158.2 133.1 %all-reduce.2.cloned.1.call-done = f32[512,512]{0,1:T(8,128)} async-done(((f32[512,512]{0,1:T(8,128)}), f32[512,512]{0,1:T(8,128)}) %all-reduce.2.cloned.1.call-update) | async-done | bytes 1048592 | tf_op jit(solution)/shard_map/psum | solution.py:73
  291.3 2.5 copy.10
  (18 shorter events, 0.1 us)
Async XLA Ops:
  7.2 1.0 copy-start
  7.2 47.8 %all-gather.2.cloned.1.call-start = ((), (), s32[]{:S(2)}) async-start(), calls=%async_computation.2 | async-start | bytes 2228224 | tf_op jit(solution)/shard_map/all_gather | solution.py:51
  10.0 58.6 %reduce-scatter.3.cloned.1.call-start = ((), (), s32[]{:S(2)}) async-start(), calls=%async_computation.3 | async-start | bytes 393216 | tf_op jit(solution)/shard_map/reduce_scatter | solution.py:52
  12.3 58.1 %copy-start.1 = (bf16[16,2,128,128]{3,2,1,0:T(8,128)(2,1)}, bf16[16,2,128,128]{3,2,1,0:T(8,128)(2,1)S(1)}, u32[]{:S(2)}) copy-start(bf16[16,2,128,128]{3,2,1,0:T(8,128)(2,1)S(1)} %bitcast_multiply_fusion) | copy-start | bytes 3145732
  12.3 45.7 %copy-start.6 = (s32[128]{0:T(128)S(1)}, s32[128]{0:T(128)}, u32[]{:S(2)}) copy-start(s32[128]{0:T(128)} %param.10) | copy-start | bytes 1540
  12.3 56.3 %copy-start.5 = (bf16[128,512]{1,0:T(8,128)(2,1)S(1)}, bf16[128,512]{1,0:T(8,128)(2,1)}, u32[]{:S(2)}) copy-start(bf16[128,512]{1,0:T(8,128)(2,1)} %param.11) | copy-start | bytes 393220
  58.0 97.0 %reduce-scatter.5.cloned.1.call-start = ((), (), s32[]{:S(2)}) async-start(), calls=%async_computation.4 | async-start | bytes 393216 | tf_op jit(solution)/shard_map/reduce_scatter | solution.py:64
  70.4 1.3 collective-permute-start
  71.8 8.4 %collective-permute-start.1 = (bf16[256,512]{1,0:T(8,128)(2,1)S(1)}, bf16[256,512]{1,0:T(8,128)(2,1)S(1)}, u32[]{:S(2)}, u32[]{:S(2)}) collective-permute-start(bf16[256,512]{1,0:T(8,128)(2,1)S(1)} %maximum_select_fusion.3), channel_id=1, source_target_pairs={{0,2},{1,3},{2,0},{3,1},{4,6},{5,7},{6,4},{7,5},{8,10},{9,11},{10,... | collective-permute-start | bytes 786440 | tf_op jit(solution)/shard_map/ppermute | solution.py:14
  80.4 13.2 %collective-permute-start.2 = (bf16[512,512]{1,0:T(8,128)(2,1)S(1)}, bf16[512,512]{1,0:T(8,128)(2,1)S(1)}, u32[]{:S(2)}, u32[]{:S(2)}) collective-permute-start(bf16[512,512]{1,0:T(8,128)(2,1)S(1)} %maximum_select_fusion.2), channel_id=1, source_target_pairs={{0,4},{1,5},{2,6},{3,7},{4,0},{5,1},{6,2},{7,3},{8,12},{9,13},{10,... | collective-permute-start | bytes 1572872 | tf_op jit(solution)/shard_map/ppermute | solution.py:14
  94.1 46.9 %collective-permute-start.3 = (bf16[1024,512]{1,0:T(8,128)(2,1)S(1)}, bf16[1024,512]{1,0:T(8,128)(2,1)S(1)}, u32[]{:S(2)}, u32[]{:S(2)}) collective-permute-start(bf16[1024,512]{1,0:T(8,128)(2,1)S(1)} %maximum_select_fusion.1), channel_id=1, source_target_pairs={{0,8},{1,9},{2,10},{3,11},{4,12},{5,13},{6,14},{7,15},{8,0},{9,1},... | collective-permute-start | bytes 3145736 | tf_op jit(solution)/shard_map/ppermute | solution.py:14
  96.5 45.1 %copy-start.2 = (bf16[16,2,128,128]{3,2,1,0:T(8,128)(2,1)S(1)}, bf16[16,2,128,128]{3,2,1,0:T(8,128)(2,1)}, u32[]{:S(2)}) copy-start(bf16[16,2,128,128]{3,2,1,0:T(8,128)(2,1)} %copy-done.1) | copy-start | bytes 3145732
  141.6 13.4 %copy-start.3 = (bf16[128,512]{1,0:T(8,128)(2,1)S(1)}, bf16[128,512]{1,0:T(8,128)(2,1)}, u32[]{:S(2)}) copy-start(bf16[128,512]{1,0:T(8,128)(2,1)} %param.6) | copy-start | bytes 393220
  143.0 148.2 %all-reduce.2.cloned.1.call-start = ((), (), s32[]{:S(2)}) async-start(), calls=%async_computation.5 | async-start | bytes 2097152 | tf_op jit(solution)/shard_map/psum | solution.py:73
  154.9 2.3 copy-start.4
Sparse Core Ops, SparseCore 0:
  10.7 44.1 all-gather.1
  58.1 10.4 reduce-scatter.2
  143.2 11.7 reduce-scatter.4
  160.6 130.6 all-reduce.1
